TPU v7x, 32 devices: a whole 2x2x4 slice. The times are simulated.
32 devices in a mesh: dp: 8 (over z, x), table: 4 (over y, core).
Axes of the slice: x: 2, y: 2, z: 4, core: 2. Of those that a mesh axis runs over, the one named last changes fastest.
Arguments:
- feature_high: int32 [20, 2048], P(None, 'dp'), may hold values from 0 to 2047
- feature_low: int32 [20, 2048], P(None, 'dp'), may hold values from 0 to 2047
- labels: int32 [2048], P('dp'), may hold values 0 or 1
- weights: float32 [4194304], P(('dp', 'table')), may hold values from -0.6 to 0.6
- history_steps: float32 [8, 4194304], P(None, ('dp', 'table')), may hold values from -46 to 46
- history_diffs: float32 [8, 4194304], P(None, ('dp', 'table')), may hold values from -198 to 198, as said below
Outputs:
- direction: float32 [4194304], P(('dp', 'table'))
Inputs may be any that keep to these rules, and one draw needn't show every extreme that they name: Each entry of history_diffs has the sign of the matching entry of history_steps and 0.2 to 4.3 times its magnitude.
All inputs are finite; a program needn't handle non-finite values. No bound on the sum of `labels` on one device may be relied on, other than what follows from the above.
Results may differ from a plain program's by a relative error of at most 0.0001.
Values sent between devices are 32-bit elements; how exact they have to be, the bound alone decides.
A program may use at most 64 MiB of HBM per device.

v0:
```python
import jax
import jax.numpy as jnp
from jax import lax
from jax.sharding import PartitionSpec as P

TABLE = 4194304
HASHES = 4
high_mult = (40503, 96469, 255361, 362443)
low_mult = (2053, 6151, 12289, 98317)
slot_mult = (1543, 3079, 769, 3457)
shifts = (0, 1048573, 2097143, 3145727)
l2_weight = 1.0


def hashed(feature_high, feature_low, number):
    slot_index = jnp.arange(feature_high.shape[0], dtype=jnp.int32)[:, None]
    part_high = feature_high * high_mult[number] % TABLE
    part_low = feature_low * low_mult[number] % TABLE
    return (part_high + part_low + slot_index * slot_mult[number] + shifts[number]) % TABLE


def local(feature_high, feature_low, labels, weights, history_steps, history_diffs):
    width = weights.shape[0]
    shard_count = lax.axis_size("table")
    column = lax.axis_index("table")
    gathered = lax.all_gather(weights, "dp", axis=0, tiled=True)
    margin = jnp.zeros((feature_high.shape[1],), jnp.float32)
    owned_list = []
    position_list = []
    for number in range(HASHES):
        indices = hashed(feature_high, feature_low, number)
        blocks = indices // width
        owned = blocks % shard_count == column
        position = blocks // shard_count * width + indices % width
        owned_list.append(owned)
        position_list.append(position)
        margin = margin + jnp.sum(jnp.where(owned, gathered[position], 0.0), axis=0)
    margin = lax.psum(margin, "table")
    residual = jax.nn.sigmoid(margin) - labels.astype(jnp.float32)
    all_positions = jnp.concatenate([place.reshape(-1) for place in position_list])
    all_terms = jnp.concatenate(
        [jnp.where(owned, residual[None, :], 0.0).reshape(-1) for owned in owned_list]
    )
    partial_grad = jnp.zeros(gathered.shape, jnp.float32).at[all_positions].add(all_terms)
    summed = lax.psum(partial_grad, "dp")
    mine = lax.dynamic_slice_in_dim(summed, lax.axis_index("dp") * width, width)
    gradient = mine + l2_weight * weights
    memory = history_steps.shape[0]
    newest = memory - 1
    pair_sums, newest_square = lax.psum(
        (
            jnp.sum(history_steps * history_diffs, axis=1),
            jnp.sum(history_diffs[newest] * history_diffs[newest]),
        ),
        ("dp", "table"),
    )
    inverse = 1.0 / pair_sums
    current = gradient
    alphas = [None] * memory
    for which in reversed(range(memory)):
        alphas[which] = inverse[which] * lax.psum(
            jnp.sum(history_steps[which] * current), ("dp", "table")
        )
        current = current - alphas[which] * history_diffs[which]
    current = pair_sums[newest] / newest_square * current
    for which in range(memory):
        correction = inverse[which] * lax.psum(
            jnp.sum(history_diffs[which] * current), ("dp", "table")
        )
        current = current + (alphas[which] - correction) * history_steps[which]
    return -current


def solution(mesh):
    placed = (
        P(None, "dp"),
        P(None, "dp"),
        P("dp"),
        P(("dp", "table")),
        P(None, ("dp", "table")),
        P(None, ("dp", "table")),
    )
    return jax.shard_map(
        local, mesh=mesh, in_specs=placed, out_specs=P(("dp", "table")), check_vma=False
    )
```

profile of v0, /device:TPU:0, one launch (start us, length us, event | category | flops | bytes accessed | tf_op | source)
XLA Modules:
  0.0 1326.4 jit_solution(4070910795745092147)
XLA Ops:
  6.5 0.7 all-gather.2.cloned.1.call-update
  7.3 1.1 compare_select_fusion.1
  8.8 76.8 %all-gather.2.cloned.1.call-done = f32[1048576]{0:T(1024)} async-done(((f32[131072]{0:T(1024)}), f32[1048576]{0:T(1024)}) %all-gather.2.cloned.1.call-update) | async-done | bytes 4194320 | tf_op jit(solution)/shard_map/all_gather | solution.py:26
  85.6 60.4 %gather_fusion.3 = f32[5120]{0:T(1024)S(1)} fusion(f32[1048576]{0:T(1024)} %all-gather.2.cloned.1.call-done, s32[5120]{0:T(1024)S(1)} %broadcast_clamp_fusion), kind=kCustom, calls=%fused_computation.3 | custom fusion | bytes 61440 | tf_op jit(solution)/shard_map/gather | solution.py:37
  146.0 60.4 %gather_fusion.1 = f32[5120]{0:T(1024)S(1)} fusion(f32[1048576]{0:T(1024)} %all-gather.2.cloned.1.call-done, s32[5120]{0:T(1024)S(1)} %broadcast_clamp_fusion.2), kind=kCustom, calls=%fused_computation.1 | custom fusion | bytes 61440 | tf_op jit(solution)/shard_map/gather | solution.py:37
  206.5 60.4 %gather_fusion = f32[5120]{0:T(1024)S(1)} fusion(f32[1048576]{0:T(1024)} %all-gather.2.cloned.1.call-done, s32[5120]{0:T(1024)S(1)} %broadcast_clamp_fusion.3), kind=kCustom, calls=%fused_computation | custom fusion | bytes 61440 | tf_op jit(solution)/shard_map/gather | solution.py:37
  266.9 60.4 %gather_fusion.2 = f32[5120]{0:T(1024)S(1)} fusion(f32[1048576]{0:T(1024)} %all-gather.2.cloned.1.call-done, s32[5120]{0:T(1024)S(1)} %broadcast_clamp_fusion.1), kind=kCustom, calls=%fused_computation.2 | custom fusion | bytes 61440 | tf_op jit(solution)/shard_map/gather | solution.py:37
  327.5 5.7 psum.142
  333.3 109.3 %scatter_custom_fusion = f32[1048576]{0:T(1024)} fusion(s32[20480]{0:T(1024)S(1)} %bitcast.84, f32[20480]{0:T(1024)S(1)} %pad_maximum_fusion, f32[]{:T(128)} %constant.207.clone.1), kind=kCustom, calls=%fused_computation.6 | custom fusion | flops 20480 | bytes 4194308 | tf_op jit(solution)/shard_map/scatter-add | solution.py:44
  442.6 16.4 %fusion.62 = (f32[1,131072]{1,0:T(1,128)S(1)}, f32[1,131072]{1,0:T(1,128)}, f32[1,131072]{1,0:T(1,128)S(1)}, f32[1,131072]{1,0:T(1,128)}, f32[1,131072]{1,0:T(1,...) fusion(f32[8,131072]{1,0:T(8,128)} %param.10), kind=kLoop, calls=%fused_computation.207 | loop fusion | bytes 8388608 | tf_op jit(solution)/shard_map/slice | solution.py:62
  459.1 4.8 multiply_reduce_fusion
  463.9 133.7 %all-reduce.4.cloned.1.call-done = f32[1048576]{0:T(1024)} async-done(((f32[1048576]{0:T(1024)}), f32[1048576]{0:T(1024)}) %all-reduce.4.cloned.1.call-update) | async-done | bytes 4194320 | tf_op jit(solution)/shard_map/psum | solution.py:45
  597.7 1.8 multiply_reduce_fusion.16
  599.4 16.6 %fusion.61 = (f32[1,131072]{1,0:T(1,128)}, f32[1,131072]{1,0:T(1,128)S(1)}, f32[1,131072]{1,0:T(1,128)}, f32[1,131072]{1,0:T(1,128)S(1)}, f32[1,131072]{1,0:T(1,...) fusion(f32[8,131072]{1,0:T(8,128)} %param.11), kind=kLoop, calls=%fused_computation.206 | loop fusion | bytes 8388608 | tf_op jit(solution)/shard_map/slice | solution.py:64
  616.0 39.4 %all-reduce.1 = (f32[8]{0:T(128)S(1)}, f32[]{:T(128)}) all-reduce(f32[8]{0:T(128)S(1)} %multiply_reduce_fusion, f32[]{:T(128)} %multiply_reduce_fusion.16), channel_id=1, replica_groups=mesh['dp'=8,'table'=4] {'dp','table'}, use_global_device_ids=true, to_apply=%region_1.2 | all-reduce | flops 9 | bytes 72 | tf_op jit(solution)/shard_map/psum | solution.py:50
  655.4 0.7 fusion.63
  657.3 3.1 multiply_reduce_fusion.15
  660.4 40.3 %psum.145 = f32[]{:T(128)} all-reduce(f32[]{:T(128)} %get-tuple-element.23), channel_id=1, replica_groups=mesh['dp'=8,'table'=4] {'dp','table'}, use_global_device_ids=true, to_apply=%region_14.15 | all-reduce | flops 1 | bytes 8 | tf_op jit(solution)/shard_map/psum | solution.py:61
  701.9 1.9 multiply_reduce_fusion.14
  703.8 40.7 %psum.146 = f32[]{:T(128)} all-reduce(f32[]{:T(128)} %multiply_reduce_fusion.14), channel_id=1, replica_groups=mesh['dp'=8,'table'=4] {'dp','table'}, use_global_device_ids=true, to_apply=%region_16.17 | all-reduce | flops 1 | bytes 8 | tf_op jit(solution)/shard_map/psum | solution.py:61
  745.8 2.9 multiply_reduce_fusion.13
  748.7 40.4 %psum.147 = f32[]{:T(128)} all-reduce(f32[]{:T(128)} %get-tuple-element.21), channel_id=1, replica_groups=mesh['dp'=8,'table'=4] {'dp','table'}, use_global_device_ids=true, to_apply=%region_18.19 | all-reduce | flops 1 | bytes 8 | tf_op jit(solution)/shard_map/psum | solution.py:61
  790.4 1.9 multiply_reduce_fusion.12
  792.3 40.6 %psum.148 = f32[]{:T(128)} all-reduce(f32[]{:T(128)} %multiply_reduce_fusion.12), channel_id=1, replica_groups=mesh['dp'=8,'table'=4] {'dp','table'}, use_global_device_ids=true, to_apply=%region_20.21 | all-reduce | flops 1 | bytes 8 | tf_op jit(solution)/shard_map/psum | solution.py:61
  834.2 3.0 multiply_reduce_fusion.11
  837.1 40.3 %psum.149 = f32[]{:T(128)} all-reduce(f32[]{:T(128)} %get-tuple-element.19), channel_id=1, replica_groups=mesh['dp'=8,'table'=4] {'dp','table'}, use_global_device_ids=true, to_apply=%region_22.23 | all-reduce | flops 1 | bytes 8 | tf_op jit(solution)/shard_map/psum | solution.py:61
  878.7 1.8 multiply_reduce_fusion.10
  880.6 0.7 slice.50
  881.2 40.6 %psum.150 = f32[]{:T(128)} all-reduce(f32[]{:T(128)} %multiply_reduce_fusion.10), channel_id=1, replica_groups=mesh['dp'=8,'table'=4] {'dp','table'}, use_global_device_ids=true, to_apply=%region_24.25 | all-reduce | flops 1 | bytes 8 | tf_op jit(solution)/shard_map/psum | solution.py:61
  923.1 2.9 multiply_reduce_fusion.9
  926.0 40.2 %all-reduce = (f32[]{:T(128)}, f32[]{:T(128)}) all-reduce(f32[]{:T(128)} %get-tuple-element.17, f32[]{:T(128)} %get-tuple-element.61), channel_id=1, replica_groups=mesh['dp'=8,'table'=4] {'dp','table'}, use_global_device_ids=true, to_apply=%region_26.27 | all-reduce | flops 2 | bytes 16 | tf_op jit(solution)/shard_map/psum | solution.py:61
  968.8 1.9 multiply_reduce_fusion.8
  970.7 40.6 %psum.152 = f32[]{:T(128)} all-reduce(f32[]{:T(128)} %multiply_reduce_fusion.8), channel_id=1, replica_groups=mesh['dp'=8,'table'=4] {'dp','table'}, use_global_device_ids=true, to_apply=%region_28.29 | all-reduce | flops 1 | bytes 8 | tf_op jit(solution)/shard_map/psum | solution.py:67
  1012.5 3.1 multiply_reduce_fusion.7
  1015.6 40.1 %psum.153 = f32[]{:T(128)} all-reduce(f32[]{:T(128)} %get-tuple-element.15), channel_id=1, replica_groups=mesh['dp'=8,'table'=4] {'dp','table'}, use_global_device_ids=true, to_apply=%region_30.31 | all-reduce | flops 1 | bytes 8 | tf_op jit(solution)/shard_map/psum | solution.py:67
  1056.9 1.9 multiply_reduce_fusion.6
  1058.8 40.7 %psum.154 = f32[]{:T(128)} all-reduce(f32[]{:T(128)} %multiply_reduce_fusion.6), channel_id=1, replica_groups=mesh['dp'=8,'table'=4] {'dp','table'}, use_global_device_ids=true, to_apply=%region_32.33 | all-reduce | flops 1 | bytes 8 | tf_op jit(solution)/shard_map/psum | solution.py:67
  1100.8 2.9 multiply_reduce_fusion.5
  1103.7 40.1 %psum.155 = f32[]{:T(128)} all-reduce(f32[]{:T(128)} %get-tuple-element.13), channel_id=1, replica_groups=mesh['dp'=8,'table'=4] {'dp','table'}, use_global_device_ids=true, to_apply=%region_34.35 | all-reduce | flops 1 | bytes 8 | tf_op jit(solution)/shard_map/psum | solution.py:67
  1145.3 1.9 multiply_reduce_fusion.4
  1147.2 40.7 %psum.156 = f32[]{:T(128)} all-reduce(f32[]{:T(128)} %multiply_reduce_fusion.4), channel_id=1, replica_groups=mesh['dp'=8,'table'=4] {'dp','table'}, use_global_device_ids=true, to_apply=%region_36.37 | all-reduce | flops 1 | bytes 8 | tf_op jit(solution)/shard_map/psum | solution.py:67
  1189.3 2.2 multiply_reduce_fusion.3
  1191.4 40.2 %psum.157 = f32[]{:T(128)} all-reduce(f32[]{:T(128)} %get-tuple-element.11), channel_id=1, replica_groups=mesh['dp'=8,'table'=4] {'dp','table'}, use_global_device_ids=true, to_apply=%region_38.39 | all-reduce | flops 1 | bytes 8 | tf_op jit(solution)/shard_map/psum | solution.py:67
  1233.0 0.7 multiply_reduce_fusion.2
  1233.7 40.6 %psum.158 = f32[]{:T(128)} all-reduce(f32[]{:T(128)} %multiply_reduce_fusion.2), channel_id=1, replica_groups=mesh['dp'=8,'table'=4] {'dp','table'}, use_global_device_ids=true, to_apply=%region_40.41 | all-reduce | flops 1 | bytes 8 | tf_op jit(solution)/shard_map/psum | solution.py:67
  1275.5 1.8 multiply_reduce_fusion.1
  1277.3 40.1 %psum.159 = f32[]{:T(128)} all-reduce(f32[]{:T(128)} %get-tuple-element.9), channel_id=1, replica_groups=mesh['dp'=8,'table'=4] {'dp','table'}, use_global_device_ids=true, to_apply=%region_42.43 | all-reduce | flops 1 | bytes 8 | tf_op jit(solution)/shard_map/psum | solution.py:67
  1318.7 0.8 add_negate_fusion
  (49 shorter events, 0.6 us)
Async XLA Ops:
  6.5 79.1 %all-gather.2.cloned.1.call-start = ((), (), s32[]{:S(2)}) async-start(), calls=%async_computation | async-start | bytes 4718592 | tf_op jit(solution)/shard_map/all_gather | solution.py:26
  7.3 590.4 %all-reduce.4.cloned.1.call-start = ((), (), s32[]{:S(2)}) async-start(), calls=%async_computation.1 | async-start | bytes 8388608 | tf_op jit(solution)/shard_map/psum | solution.py:45
  266.9 66.3 %copy-start.4 = (s32[256]{0:T(256)S(1)}, s32[256]{0:T(256)}, u32[]{:S(2)}) copy-start(s32[256]{0:T(256)} %param.8) | copy-start | bytes 3076
  459.1 138.6 %copy-start = (f32[1,131072]{1,0:T(1,128)}, f32[1,131072]{1,0:T(1,128)S(1)}, u32[]{:S(2)}) copy-start(f32[1,131072]{1,0:T(1,128)S(1)} %get-tuple-element.59) | copy-start | bytes 1572868
  459.1 138.6 %copy-start.3 = (f32[131072]{0:T(1024)S(1)}, f32[131072]{0:T(1024)}, u32[]{:S(2)}) copy-start(f32[131072]{0:T(1024)} %param.9) | copy-start | bytes 1572868
  1100.8 174.7 %copy-start.2 = (f32[1,131072]{1,0:T(1,128)S(1)}, f32[1,131072]{1,0:T(1,128)}, u32[]{:S(2)}) copy-start(f32[1,131072]{1,0:T(1,128)} %get-tuple-element.58) | copy-start | bytes 1572868
  1145.3 173.4 %copy-start.1 = (f32[1,131072]{1,0:T(1,128)S(1)}, f32[1,131072]{1,0:T(1,128)}, u32[]{:S(2)}) copy-start(f32[1,131072]{1,0:T(1,128)} %copy-done) | copy-start | bytes 1572868
Sparse Core Ops, SparseCore 0:
  9.5 76.0 all-gather.1
  442.8 154.8 all-reduce.3
where the time goes:
time: 1340 us; the launch traced here: 1330 us
  blocking collectives  651 us (49%)
  local copies, waits for them, and re-layouts  276 us (21%)
  waiting for transfers between devices  211 us (16%)
  other arithmetic  152 us (11%)
  between operations  35.7 us (3%)
    psum x8, blocking collectives, local(): lax.psum(jnp.sum(history_diffs[which] * current), ('dp', 'table'))  323 us
    psum x7, blocking collectives, local(): lax.psum(jnp.sum(history_steps[which] * current), ('dp', 'table'))  283 us
    gather x8, local copies, waits for them, and re-layouts, local(): margin = margin + jnp.sum(jnp.where(owned, gathered[position], 0.0), axis=0)  242 us
    psum x1, waiting for transfers between devices, local(): summed = lax.psum(partial_grad, 'dp')  134 us
    scatter-add x1, other arithmetic, local(): jnp.zeros(gathered.shape, jnp.float32).at[all_positions].add(all_terms)  109 us
    all_gather x1, waiting for transfers between devices, local(): gathered = lax.all_gather(weights, 'dp', axis=0, tiled=True)  76.8 us
    psum x1, blocking collectives, local(): lax.psum((jnp.sum(history_steps * history_diffs, axis=1), jnp.sum(history...  39.4 us
  transfers between devices with their start and end apart: 2, of which 2 were waited for; matrix products, arithmetic and copies ran while one was open for 2% of the time, Pallas kernels for 0%

commit v1 on v0

--- a/solution.py
+++ b/solution.py
@@ -23,7 +23,10 @@
     width = weights.shape[0]
     shard_count = lax.axis_size("table")
     column = lax.axis_index("table")
-    gathered = lax.all_gather(weights, "dp", axis=0, tiled=True)
+    devices = lax.axis_size("dp")
+    parts = jnp.stack([weights for _ in range(devices)])
+    parts = lax.all_to_all(parts, "dp", split_axis=0, concat_axis=0)
+    gathered = jnp.concatenate(parts, axis=0)
     margin = jnp.zeros((feature_high.shape[1],), jnp.float32)
     owned_list = []
     position_list = []

time: 1340 us -> 1360 us (1.015)
  waiting for transfers between devices: 211 us -> 227 us
    all_to_all x0 -> x1, waiting for transfers between devices: none -> 92.5 us  [local(): parts = lax.all_to_all(parts, 'dp', split_axis=0, concat_axis=0)]
    all_gather x1 -> x0, waiting for transfers between devices: 76.8 us -> none  [local(): gathered = lax.all_gather(weights, 'dp', axis=0, tiled=True)]
where the time goes in v1:
time: 1360 us; the launch traced here: 1350 us
  blocking collectives  651 us (48%)
  local copies, waits for them, and re-layouts  281 us (21%)
  waiting for transfers between devices  227 us (17%)
  other arithmetic  151 us (11%)
  between operations  35.7 us (3%)
    psum x8, blocking collectives, local(): lax.psum(jnp.sum(history_diffs[which] * current), ('dp', 'table'))  323 us
    psum x7, blocking collectives, local(): lax.psum(jnp.sum(history_steps[which] * current), ('dp', 'table'))  283 us
    gather x8, local copies, waits for them, and re-layouts, local(): margin = margin + jnp.sum(jnp.where(owned, gathered[position], 0.0), axis=0)  242 us
    psum x1, waiting for transfers between devices, local(): summed = lax.psum(partial_grad, 'dp')  134 us
    scatter-add x1, other arithmetic, local(): jnp.zeros(gathered.shape, jnp.float32).at[all_positions].add(all_terms)  109 us
    all_to_all x1, waiting for transfers between devices, local(): parts = lax.all_to_all(parts, 'dp', split_axis=0, concat_axis=0)  92.5 us
    psum x1, blocking collectives, local(): lax.psum((jnp.sum(history_steps * history_diffs, axis=1), jnp.sum(history...  39.4 us
  transfers between devices with their start and end apart: 2, of which 2 were waited for; matrix products, arithmetic and copies ran while one was open for 2% of the time, Pallas kernels for 0%

profile of v1, /device:TPU:0, one launch (start us, length us, event | category | flops | bytes accessed | tf_op | source)
XLA Modules:
  0.0 1354.0 jit_solution(14916371349976675883)
XLA Ops:
  6.5 5.2 stack.2
  11.7 7.4 all-to-all-start
  19.9 92.5 %all-to-all-done = f32[8,1,131072]{2,1,0:T(1,128)} async-done(((f32[8,1,131072]{2,1,0:T(1,128)}), f32[8,1,131072]{2,1,0:T(1,128)}, u32[]{:S(2)}, u32[]{:S(2)}) %all-to-all-start) | async-done | bytes 4194336 | tf_op jit(solution)/shard_map/all_to_all | solution.py:28
  112.4 60.4 %gather_fusion.3 = f32[5120]{0:T(1024)S(1)} fusion(f32[1048576]{0:T(1024)} %bitcast.3, s32[5120]{0:T(1024)S(1)} %broadcast_clamp_fusion), kind=kCustom, calls=%fused_computation.3 | custom fusion | bytes 61440 | tf_op jit(solution)/shard_map/gather | solution.py:40
  172.8 60.4 %gather_fusion.2 = f32[5120]{0:T(1024)S(1)} fusion(f32[1048576]{0:T(1024)} %bitcast.3, s32[5120]{0:T(1024)S(1)} %broadcast_clamp_fusion.1), kind=kCustom, calls=%fused_computation.2 | custom fusion | bytes 61440 | tf_op jit(solution)/shard_map/gather | solution.py:40
  233.2 60.4 %gather_fusion.1 = f32[5120]{0:T(1024)S(1)} fusion(f32[1048576]{0:T(1024)} %bitcast.3, s32[5120]{0:T(1024)S(1)} %broadcast_clamp_fusion.2), kind=kCustom, calls=%fused_computation.1 | custom fusion | bytes 61440 | tf_op jit(solution)/shard_map/gather | solution.py:40
  293.7 60.4 %gather_fusion = f32[5120]{0:T(1024)S(1)} fusion(f32[1048576]{0:T(1024)} %bitcast.3, s32[5120]{0:T(1024)S(1)} %broadcast_clamp_fusion.3), kind=kCustom, calls=%fused_computation | custom fusion | bytes 61440 | tf_op jit(solution)/shard_map/gather | solution.py:40
  354.3 5.7 psum.142
  360.1 109.3 %scatter_custom_fusion = f32[1048576]{0:T(1024)} fusion(s32[20480]{0:T(1024)S(1)} %bitcast.85, f32[20480]{0:T(1024)S(1)} %pad_maximum_fusion, f32[]{:T(128)} %constant.207.clone.1), kind=kCustom, calls=%fused_computation.6 | custom fusion | flops 20480 | bytes 4194308 | tf_op jit(solution)/shard_map/scatter-add | solution.py:47
  469.4 16.4 %fusion.62 = (f32[1,131072]{1,0:T(1,128)S(1)}, f32[1,131072]{1,0:T(1,128)}, f32[1,131072]{1,0:T(1,128)S(1)}, f32[1,131072]{1,0:T(1,128)}, f32[1,131072]{1,0:T(1,...) fusion(f32[8,131072]{1,0:T(8,128)} %param.10), kind=kLoop, calls=%fused_computation.207 | loop fusion | bytes 8388608 | tf_op jit(solution)/shard_map/slice | solution.py:65
  485.8 4.9 multiply_reduce_fusion
  490.7 134.4 %all-reduce.4.cloned.1.call-done = f32[1048576]{0:T(1024)} async-done(((f32[1048576]{0:T(1024)}), f32[1048576]{0:T(1024)}) %all-reduce.4.cloned.1.call-update) | async-done | bytes 4194320 | tf_op jit(solution)/shard_map/psum | solution.py:48
  625.2 1.8 multiply_reduce_fusion.16
  626.9 16.6 %fusion.61 = (f32[1,131072]{1,0:T(1,128)}, f32[1,131072]{1,0:T(1,128)S(1)}, f32[1,131072]{1,0:T(1,128)}, f32[1,131072]{1,0:T(1,128)S(1)}, f32[1,131072]{1,0:T(1,...) fusion(f32[8,131072]{1,0:T(8,128)} %param.11), kind=kLoop, calls=%fused_computation.206 | loop fusion | bytes 8388608 | tf_op jit(solution)/shard_map/slice | solution.py:67
  643.5 39.4 %all-reduce.1 = (f32[8]{0:T(128)S(1)}, f32[]{:T(128)}) all-reduce(f32[8]{0:T(128)S(1)} %multiply_reduce_fusion, f32[]{:T(128)} %multiply_reduce_fusion.16), channel_id=1, replica_groups=mesh['dp'=8,'table'=4] {'dp','table'}, use_global_device_ids=true, to_apply=%region_1.2 | all-reduce | flops 9 | bytes 72 | tf_op jit(solution)/shard_map/psum | solution.py:53
  682.9 0.7 fusion.63
  684.8 3.1 multiply_reduce_fusion.15
  687.9 40.3 %psum.145 = f32[]{:T(128)} all-reduce(f32[]{:T(128)} %get-tuple-element.23), channel_id=1, replica_groups=mesh['dp'=8,'table'=4] {'dp','table'}, use_global_device_ids=true, to_apply=%region_14.15 | all-reduce | flops 1 | bytes 8 | tf_op jit(solution)/shard_map/psum | solution.py:64
  729.4 1.9 multiply_reduce_fusion.14
  731.3 40.5 %psum.146 = f32[]{:T(128)} all-reduce(f32[]{:T(128)} %multiply_reduce_fusion.14), channel_id=1, replica_groups=mesh['dp'=8,'table'=4] {'dp','table'}, use_global_device_ids=true, to_apply=%region_16.17 | all-reduce | flops 1 | bytes 8 | tf_op jit(solution)/shard_map/psum | solution.py:64
  773.1 2.9 multiply_reduce_fusion.13
  776.0 40.4 %psum.147 = f32[]{:T(128)} all-reduce(f32[]{:T(128)} %get-tuple-element.21), channel_id=1, replica_groups=mesh['dp'=8,'table'=4] {'dp','table'}, use_global_device_ids=true, to_apply=%region_18.19 | all-reduce | flops 1 | bytes 8 | tf_op jit(solution)/shard_map/psum | solution.py:64
  817.7 1.9 multiply_reduce_fusion.12
  819.6 40.6 %psum.148 = f32[]{:T(128)} all-reduce(f32[]{:T(128)} %multiply_reduce_fusion.12), channel_id=1, replica_groups=mesh['dp'=8,'table'=4] {'dp','table'}, use_global_device_ids=true, to_apply=%region_20.21 | all-reduce | flops 1 | bytes 8 | tf_op jit(solution)/shard_map/psum | solution.py:64
  861.5 3.0 multiply_reduce_fusion.11
  864.5 40.3 %psum.149 = f32[]{:T(128)} all-reduce(f32[]{:T(128)} %get-tuple-element.19), channel_id=1, replica_groups=mesh['dp'=8,'table'=4] {'dp','table'}, use_global_device_ids=true, to_apply=%region_22.23 | all-reduce | flops 1 | bytes 8 | tf_op jit(solution)/shard_map/psum | solution.py:64
  906.1 1.8 multiply_reduce_fusion.10
  907.9 0.7 slice.50
  908.6 40.6 %psum.150 = f32[]{:T(128)} all-reduce(f32[]{:T(128)} %multiply_reduce_fusion.10), channel_id=1, replica_groups=mesh['dp'=8,'table'=4] {'dp','table'}, use_global_device_ids=true, to_apply=%region_24.25 | all-reduce | flops 1 | bytes 8 | tf_op jit(solution)/shard_map/psum | solution.py:64
  950.5 2.9 multiply_reduce_fusion.9
  953.3 40.4 %all-reduce = (f32[]{:T(128)}, f32[]{:T(128)}) all-reduce(f32[]{:T(128)} %get-tuple-element.17, f32[]{:T(128)} %get-tuple-element.61), channel_id=1, replica_groups=mesh['dp'=8,'table'=4] {'dp','table'}, use_global_device_ids=true, to_apply=%region_26.27 | all-reduce | flops 2 | bytes 16 | tf_op jit(solution)/shard_map/psum | solution.py:64
  996.4 1.9 multiply_reduce_fusion.8
  998.3 40.6 %psum.152 = f32[]{:T(128)} all-reduce(f32[]{:T(128)} %multiply_reduce_fusion.8), channel_id=1, replica_groups=mesh['dp'=8,'table'=4] {'dp','table'}, use_global_device_ids=true, to_apply=%region_28.29 | all-reduce | flops 1 | bytes 8 | tf_op jit(solution)/shard_map/psum | solution.py:70
  1040.1 3.1 multiply_reduce_fusion.7
  1043.2 40.1 %psum.153 = f32[]{:T(128)} all-reduce(f32[]{:T(128)} %get-tuple-element.15), channel_id=1, replica_groups=mesh['dp'=8,'table'=4] {'dp','table'}, use_global_device_ids=true, to_apply=%region_30.31 | all-reduce | flops 1 | bytes 8 | tf_op jit(solution)/shard_map/psum | solution.py:70
  1084.5 1.9 multiply_reduce_fusion.6
  1086.4 40.7 %psum.154 = f32[]{:T(128)} all-reduce(f32[]{:T(128)} %multiply_reduce_fusion.6), channel_id=1, replica_groups=mesh['dp'=8,'table'=4] {'dp','table'}, use_global_device_ids=true, to_apply=%region_32.33 | all-reduce | flops 1 | bytes 8 | tf_op jit(solution)/shard_map/psum | solution.py:70
  1128.4 2.9 multiply_reduce_fusion.5
  1131.3 40.1 %psum.155 = f32[]{:T(128)} all-reduce(f32[]{:T(128)} %get-tuple-element.13), channel_id=1, replica_groups=mesh['dp'=8,'table'=4] {'dp','table'}, use_global_device_ids=true, to_apply=%region_34.35 | all-reduce | flops 1 | bytes 8 | tf_op jit(solution)/shard_map/psum | solution.py:70
  1172.8 1.9 multiply_reduce_fusion.4
  1174.8 40.7 %psum.156 = f32[]{:T(128)} all-reduce(f32[]{:T(128)} %multiply_reduce_fusion.4), channel_id=1, replica_groups=mesh['dp'=8,'table'=4] {'dp','table'}, use_global_device_ids=true, to_apply=%region_36.37 | all-reduce | flops 1 | bytes 8 | tf_op jit(solution)/shard_map/psum | solution.py:70
  1216.8 2.2 multiply_reduce_fusion.3
  1219.0 40.2 %psum.157 = f32[]{:T(128)} all-reduce(f32[]{:T(128)} %get-tuple-element.11), channel_id=1, replica_groups=mesh['dp'=8,'table'=4] {'dp','table'}, use_global_device_ids=true, to_apply=%region_38.39 | all-reduce | flops 1 | bytes 8 | tf_op jit(solution)/shard_map/psum | solution.py:70
  1260.5 0.7 multiply_reduce_fusion.2
  1261.3 40.6 %psum.158 = f32[]{:T(128)} all-reduce(f32[]{:T(128)} %multiply_reduce_fusion.2), channel_id=1, replica_groups=mesh['dp'=8,'table'=4] {'dp','table'}, use_global_device_ids=true, to_apply=%region_40.41 | all-reduce | flops 1 | bytes 8 | tf_op jit(solution)/shard_map/psum | solution.py:70
  1303.1 1.8 multiply_reduce_fusion.1
  1304.9 40.2 %psum.159 = f32[]{:T(128)} all-reduce(f32[]{:T(128)} %get-tuple-element.9), channel_id=1, replica_groups=mesh['dp'=8,'table'=4] {'dp','table'}, use_global_device_ids=true, to_apply=%region_42.43 | all-reduce | flops 1 | bytes 8 | tf_op jit(solution)/shard_map/psum | solution.py:70
  1346.3 0.8 add_negate_fusion
  (53 shorter events, 0.9 us)
Async XLA Ops:
  11.7 7.5 copy-start.4
  11.7 7.5 copy-start.5
  11.7 100.7 %all-to-all-start = ((f32[8,1,131072]{2,1,0:T(1,128)}), f32[8,1,131072]{2,1,0:T(1,128)}, u32[]{:S(2)}, u32[]{:S(2)}) async-start(f32[8,1,131072]{2,1,0:T(1,128)} %stack.2), calls=%async_computation | async-start | bytes 8388608 | tf_op jit(solution)/shard_map/all_to_all | solution.py:28
  19.1 606.1 %all-reduce.4.cloned.1.call-start = ((), (), s32[]{:S(2)}) async-start(), calls=%async_computation.1 | async-start | bytes 8388608 | tf_op jit(solution)/shard_map/psum | solution.py:48
  293.6 66.3 %copy-start.6 = (s32[256]{0:T(256)S(1)}, s32[256]{0:T(256)}, u32[]{:S(2)}) copy-start(s32[256]{0:T(256)} %param.8) | copy-start | bytes 3076
  485.8 139.4 %copy-start = (f32[1,131072]{1,0:T(1,128)}, f32[1,131072]{1,0:T(1,128)S(1)}, u32[]{:S(2)}) copy-start(f32[1,131072]{1,0:T(1,128)S(1)} %get-tuple-element.59) | copy-start | bytes 1572868
  485.8 139.4 %copy-start.2 = (f32[131072]{0:T(1024)S(1)}, f32[131072]{0:T(1024)}, u32[]{:S(2)}) copy-start(f32[131072]{0:T(1024)} %param.9) | copy-start | bytes 1572868
  1128.4 174.7 %copy-start.3 = (f32[1,131072]{1,0:T(1,128)S(1)}, f32[1,131072]{1,0:T(1,128)}, u32[]{:S(2)}) copy-start(f32[1,131072]{1,0:T(1,128)} %get-tuple-element.58) | copy-start | bytes 1572868
  1172.8 173.5 %copy-start.1 = (f32[1,131072]{1,0:T(1,128)S(1)}, f32[1,131072]{1,0:T(1,128)}, u32[]{:S(2)}) copy-start(f32[1,131072]{1,0:T(1,128)} %copy-done) | copy-start | bytes 1572868
Sparse Core Ops, SparseCore 0:
  469.5 155.6 all-reduce.3
